TPU v7x, 512 devices: a whole 4x4x16 slice. The times are simulated.
512 devices in a mesh: section: 8 (over x, core), tm: 16 (over z_hi, y), dp: 4 (over z_lo).
Axes of the slice: x: 4, y: 4, z: 16 (z_hi: 4, z_lo: 4; z = z_hi * 4 + z_lo), core: 2. Of those that a mesh axis runs over, the one named last changes fastest.
Arguments:
- frames: bfloat16 [32, 8192, 512], P(('section', 'dp'), 'tm'), may hold values from -6 to 6
- lengths: int32 [32], P(('section', 'dp')), may hold values from 40960 to 163840, as said below
- fourth_conv: bfloat16 [3, 512, 512], P(None, ('section', 'dp')), may hold values from -0.15625 to 0.15625
- fifth_conv: bfloat16 [3, 512, 512], P(None, ('section', 'dp')), may hold values from -0.15625 to 0.15625
- sixth_conv: bfloat16 [2, 512, 512], P(None, ('section', 'dp')), may hold values from -0.1875 to 0.1875
- seventh_conv: bfloat16 [2, 512, 512], P(None, ('section', 'dp')), may hold values from -0.1875 to 0.1875
- norm_gain: float32 [512], replicated, may hold values from 0.5 to 1.5
- norm_bias: float32 [512], replicated, may hold values from -1.8 to 1.8
- project_weight: bfloat16 [512, 1920], P(None, 'tm'), may hold values from -0.25 to 0.25
- project_bias: bfloat16 [1, 1920], P(None, 'tm'), may hold values from -1.796875 to 1.796875
- position_weight: bfloat16 [16, 128, 14400], P('tm', ('section', 'dp')), may hold values from -0.046875 to 0.046875
- position_bias: float32 [1920], P('tm'), may hold values from -3 to 3
Outputs:
- encoded: bfloat16 [32, 1920, 512], P(('section', 'dp'), 'tm')
Inputs may be any that keep to these rules, and one draw needn't show every extreme that they name: `lengths`: length of each utterance in samples; some utterance of every draw fills all 8192 input frames.
All inputs are finite; a program needn't handle non-finite values.
Results may differ from a plain program's by a relative error of at most 0.012.
Values may be sent and summed in bfloat16 or wider, within the bound.
A program may use at most 64 MiB of HBM per device.

v0:
```python
import jax
import jax.numpy as jnp
from jax import lax
from jax.sharding import PartitionSpec as P

TAPS = 128


eps_norm = 1e-05


def passed_along(x, axis, by):
    length = lax.axis_size(axis)
    pairs = [(i, i + by) for i in range(length) if 0 <= i + by < length]
    return lax.ppermute(x, axis, pairs)


def layer_norm(values):
    average = jnp.mean(values, axis=-1, keepdims=True)
    centred = values - average
    spread = jnp.mean(centred * centred, axis=-1, keepdims=True)
    return centred * lax.rsqrt(spread + eps_norm)


def conv_layer(even_rows, odd_rows, weight, out_rows):
    tap_count = weight.shape[0]
    whole = lax.all_gather(weight, ("section", "dp"), axis=1, tiled=True)
    summed = jnp.dot(even_rows[:out_rows], whole[0], preferred_element_type=jnp.float32)
    summed = summed + jnp.dot(odd_rows[:out_rows], whole[1], preferred_element_type=jnp.float32)
    if tap_count == 3:
        summed = summed + jnp.dot(
            even_rows[1 : out_rows + 1], whole[2], preferred_element_type=jnp.float32
        )
    return jax.nn.gelu(layer_norm(summed), approximate=False).astype(jnp.bfloat16)


def paired_conv(current, weight, out_rows):
    paired = current.reshape(current.shape[0] // 2, 2, current.shape[1])
    return conv_layer(paired[:, 0], paired[:, 1], weight, out_rows)


def local(
    frames,
    lengths,
    fourth_conv,
    fifth_conv,
    sixth_conv,
    seventh_conv,
    norm_gain,
    norm_bias,
    project_weight,
    project_bias,
    position_weight,
    position_bias,
):
    inputs = frames[0]
    length = lengths[0]
    row_count = inputs.shape[0]
    channels = inputs.shape[1]
    sample_index = lax.axis_index("tm") * row_count + jnp.arange(row_count, dtype=jnp.int32)
    masked = jnp.where((sample_index * 20 < length)[:, None], inputs, jnp.zeros_like(inputs))
    zero_row = jnp.zeros((1, channels), jnp.bfloat16)
    current = masked
    for weight in (fourth_conv, fifth_conv, sixth_conv, seventh_conv):
        if weight.shape[0] == 3:
            next_rim = passed_along(current[:1], "tm", -1)
        else:
            next_rim = zero_row
        padded = jnp.concatenate([current, next_rim, zero_row], axis=0)
        current = paired_conv(padded, weight, current.shape[0] // 2)
    normed = (layer_norm(current.astype(jnp.float32)) * norm_gain + norm_bias).astype(jnp.bfloat16)
    shard_pieces = lax.all_gather((project_weight, project_bias), "tm", axis=1, tiled=True)
    projected = (
        jnp.dot(normed, shard_pieces[0], preferred_element_type=jnp.float32)
        + shard_pieces[1].astype(jnp.float32)
    ).astype(jnp.bfloat16)
    grouped = lax.all_to_all(projected, "tm", split_axis=1, concat_axis=0, tiled=True)
    frame_total = grouped.shape[0]
    group_width = grouped.shape[1]
    frame_index = jnp.arange(frame_total, dtype=jnp.int32)
    grouped = jnp.where((frame_index * 320 < length)[:, None], grouped, jnp.zeros_like(grouped))
    pad_rows = TAPS // 2
    padded_group = jnp.pad(grouped, ((pad_rows, pad_rows), (0, 0)))
    zeros_conv = jnp.zeros((group_width, frame_total), jnp.float32)
    shard_piece = lax.all_gather(position_weight, ("section", "dp"), axis=1, tiled=True)
    tap_total = shard_piece.shape[1]
    block_taps = min(tap_total, 16)
    kernel = shard_piece[0].reshape(tap_total, group_width, group_width)

    def one_block(counter, partial_value):
        base_tap = counter * block_taps
        window = jnp.concatenate(
            [
                lax.dynamic_slice_in_dim(padded_group, base_tap + offset, frame_total, 0)
                for offset in range(block_taps)
            ],
            axis=1,
        )
        window = window.reshape(frame_total, block_taps, group_width)
        tap_weights = lax.dynamic_slice_in_dim(kernel, counter * block_taps, block_taps, 0)
        return partial_value + lax.dot_general(
            tap_weights, window, (((0, 2), (1, 2)), ((), ())), preferred_element_type=jnp.float32
        )

    conv = lax.fori_loop(0, tap_total // block_taps, one_block, zeros_conv)
    position = jax.nn.gelu(conv + position_bias[:, None], approximate=False)
    encoded = (grouped.astype(jnp.float32).T + position).astype(jnp.bfloat16)
    return encoded[None]


def solution(mesh):
    in_specs = (
        P(("section", "dp"), "tm", None),
        P(("section", "dp")),
        P(None, ("section", "dp"), None),
        P(None, ("section", "dp"), None),
        P(None, ("section", "dp"), None),
        P(None, ("section", "dp"), None),
        P(),
        P(),
        P(None, "tm"),
        P(None, "tm"),
        P("tm", ("section", "dp"), None),
        P("tm"),
    )
    out_specs = P(("section", "dp"), "tm", None)
    return jax.shard_map(local, mesh=mesh, in_specs=in_specs, out_specs=out_specs, check_vma=False)
```

profile of v0, /device:TPU:7, one launch (start us, length us, event | category | flops | bytes accessed | tf_op | source)
XLA Modules:
  0.0 631.7 jit_solution(15900716552288569270)
XLA Ops:
  6.5 0.7 all-gather.7.cloned.1.call-update
  7.3 0.7 all-gather.9.cloned.1.call-update
  8.1 0.7 all-gather.11.cloned.1.call-update
  8.8 0.5 all-gather.13.cloned.1.call-update
  9.4 0.5 all-gather.15.cloned.1.call-update
  10.6 1.2 bitcast_select_fusion
  11.8 1.3 collective-permute-start
  13.1 1.8 copy.48
  14.9 1.3 dynamic-slice
  16.9 0.9 dynamic-update-slice
  17.8 0.3 reshape.109
  18.1 0.9 fusion.78
  19.0 84.2 %all-gather.7.cloned.1.call-done = bf16[3,512,512]{2,1,0:T(8,128)(2,1)} async-done(((bf16[3,16,512]{2,1,0:T(8,128)(2,1)}), bf16[3,512,512]{2,1,0:T(8,128)(2,1)}) %all-gather.7.cloned.1.call-update) | async-done | bytes 1572880 | tf_op jit(solution)/shard_map/all_gather | solution.py:27
  103.3 1.3 fusion.10
  104.6 1.3 convolution_add_fusion.2
  106.0 1.4 fusion.82
  107.4 0.2 multiply_reduce_fusion
  107.6 1.3 fusion.6
  109.0 1.3 collective-permute-start.1
  110.3 48.9 %all-reduce.3 = bf16[1920]{0:T(1024)(128)(2,1)S(1)} all-reduce(bf16[1920]{0:T(1024)(128)(2,1)S(1)} %dynamic-update-slice), channel_id=1, replica_groups=mesh['section'=8,'tm'=16,'dp'=4] {'tm'}, use_global_device_ids=true, to_apply=%add.3 | all-reduce | flops 1920 | bytes 7680
  159.2 0.1 reshape.110
  159.4 0.5 fusion.79
  159.8 37.3 %all-gather.9.cloned.1.call-done = bf16[3,512,512]{2,1,0:T(8,128)(2,1)} async-done(((bf16[3,16,512]{2,1,0:T(8,128)(2,1)}), bf16[3,512,512]{2,1,0:T(8,128)(2,1)}) %all-gather.9.cloned.1.call-update) | async-done | bytes 1572880 | tf_op jit(solution)/shard_map/all_gather | solution.py:27
  197.2 1.3 fusion.9
  198.4 1.3 convolution_add_fusion.4
  199.7 1.4 fusion.83
  201.1 0.2 multiply_reduce_fusion.1
  201.3 0.7 fusion.20
  202.1 0.2 fusion.80
  202.3 86.5 %all-gather.11.cloned.1.call-done = bf16[2,512,512]{2,1,0:T(8,128)(2,1)} async-done(((bf16[2,16,512]{2,1,0:T(8,128)(2,1)}), bf16[2,512,512]{2,1,0:T(8,128)(2,1)}) %all-gather.11.cloned.1.call-update) | async-done | bytes 1048592 | tf_op jit(solution)/shard_map/all_gather | solution.py:27
  288.7 1.3 fusion.8
  290.0 1.4 fusion.84
  291.4 0.2 multiply_reduce_fusion.2
  291.6 0.4 fusion.47
  292.1 89.1 %all-gather.13.cloned.1.call-done = bf16[2,512,512]{2,1,0:T(8,128)(2,1)} async-done(((bf16[2,16,512]{2,1,0:T(8,128)(2,1)}), bf16[2,512,512]{2,1,0:T(8,128)(2,1)}) %all-gather.13.cloned.1.call-update) | async-done | bytes 1048592 | tf_op jit(solution)/shard_map/all_gather | solution.py:27
  381.2 1.2 fusion.7
  382.4 1.4 fusion.85
  383.8 0.2 multiply_reduce_fusion.3
  384.0 0.3 convert_reduce_fusion
  384.4 0.2 fusion.58
  384.6 93.1 %all-gather.15.cloned.1.call-done = bf16[512,1920]{0,1:T(8,128)(2,1)} async-done(((bf16[512,120]{0,1:T(8,128)(2,1)}), bf16[512,1920]{0,1:T(8,128)(2,1)}) %all-gather.15.cloned.1.call-update) | async-done | bytes 1966096 | tf_op jit(solution)/shard_map/all_gather | solution.py:72
  477.6 2.2 fusion.3
  479.9 0.3 all_to_all.14
  480.2 0.7 copy.47
  480.9 5.9 all-to-all-start
  486.9 14.1 %all-to-all-done = bf16[32,16,120]{2,0,1:T(8,128)(2,1)S(1)} async-done(((bf16[32,16,120]{2,0,1:T(8,128)(2,1)}), bf16[32,16,120]{2,0,1:T(8,128)(2,1)S(1)}, u32[]{:S(2)}, u32[]{:S(2)}) %all-to-all-start) | async-done | bytes 122912 | tf_op jit(solution)/shard_map/all_to_all | solution.py:77
  501.0 0.1 bitcast_select_fusion.1
  501.1 0.1 copy.64
  501.3 0.1 pad.6.clone
  501.4 72.0 %all-gather.17.cloned.1.call-done = bf16[1,128,14400]{2,0,1:T(2,128)(2,1)} async-done(((bf16[1,4,14400]{2,0,1:T(2,128)(2,1)}), bf16[1,128,14400]{2,0,1:T(2,128)(2,1)}) %all-gather.17.cloned.1.call-update) | async-done | bytes 3686416 | tf_op jit(solution)/shard_map/all_gather | solution.py:85
  573.4 15.3 %copy.49 = bf16[1,128,14400]{1,2,0:T(8,128)(2,1)} copy(bf16[1,128,14400]{2,0,1:T(2,128)(2,1)} %all-gather.17.cloned.1.call-done) | data formatting | bytes 7372800 | tf_op jit(solution)/shard_map/all_gather | solution.py:85
  588.7 6.3 copy.50
  595.0 28.3 %while.16 = (s32[]{:T(128)}, f32[120,512]{1,0:T(8,128)S(1)}, bf16[128,120,120]{2,1,0:T(8,128)(2,1)}, bf16[640,120]{0,1:T(8,128)(2,1)S(1)}, s32[]{:T(128)}, /*ind...) while((s32[]{:T(128)}, f32[120,512]{1,0:T(8,128)S(1)}, ...), condition=%wide.region_11.12_spmd.clone, body=%wide.region_10.11_spmd.clone.sunk | while | flops 236052544 | bytes 6882444 | solution.py:105
  596.9 1.5 fusion.93
  600.5 1.5 fusion.93
  604.0 1.5 fusion.93
  607.6 1.5 fusion.93
  611.1 1.5 fusion.93
  614.6 1.5 fusion.93
  618.2 1.5 fusion.93
  621.7 1.5 fusion.93
  623.3 0.1 copy.52
  623.4 0.6 fusion.55
  624.1 0.8 copy.53
  (168 shorter events, 14.2 us)
Async XLA Ops:
  6.5 96.7 %all-gather.7.cloned.1.call-start = ((), (), s32[]{:S(2)}) async-start(), calls=%async_computation.1 | async-start | bytes 1622016 | tf_op jit(solution)/shard_map/all_gather | solution.py:27
  7.3 189.9 %all-gather.9.cloned.1.call-start = ((), (), s32[]{:S(2)}) async-start(), calls=%async_computation.2 | async-start | bytes 1622016 | tf_op jit(solution)/shard_map/all_gather | solution.py:27
  8.0 280.7 %all-gather.11.cloned.1.call-start = ((), (), s32[]{:S(2)}) async-start(), calls=%async_computation.3 | async-start | bytes 1081344 | tf_op jit(solution)/shard_map/all_gather | solution.py:27
  8.7 372.5 %all-gather.13.cloned.1.call-start = ((), (), s32[]{:S(2)}) async-start(), calls=%async_computation.4 | async-start | bytes 1081344 | tf_op jit(solution)/shard_map/all_gather | solution.py:27
  9.3 468.3 %all-gather.15.cloned.1.call-start = ((), (), s32[]{:S(2)}) async-start(), calls=%async_computation.5 | async-start | bytes 2088960 | tf_op jit(solution)/shard_map/all_gather | solution.py:72
  9.9 563.5 %all-gather.17.cloned.1.call-start = ((), (), s32[]{:S(2)}) async-start(), calls=%async_computation.6 | async-start | bytes 7636992 | tf_op jit(solution)/shard_map/all_gather | solution.py:85
  11.8 5.9 collective-permute-start
  109.0 50.2 %collective-permute-start.1 = (bf16[1,512]{1,0:T(2,128)(2,1)S(1)}, bf16[1,512]{1,0:T(2,128)(2,1)S(1)}, u32[]{:S(2)}, u32[]{:S(2)}) collective-permute-start(bf16[1,512]{1,0:T(2,128)(2,1)S(1)} %slice.153), channel_id=1, source_target_pairs={{4,0},{8,4},{12,8},{16,12},{20,16},{24,20},{28,24},{32,28},{36,32}... | collective-permute-start | bytes 3080 | tf_op jit(solution)/shard_map/ppermute | solution.py:15
  288.7 188.9 %copy-start = (f32[512]{0:T(512)S(1)}, f32[512]{0:T(512)}, u32[]{:S(2)}) copy-start(f32[512]{0:T(512)} %param.21) | copy-start | bytes 6148
  288.7 188.9 %copy-start.1 = (f32[512]{0:T(512)S(1)}, f32[512]{0:T(512)}, u32[]{:S(2)}) copy-start(f32[512]{0:T(512)} %param.20) | copy-start | bytes 6148
  480.9 20.1 %all-to-all-start = ((bf16[32,16,120]{2,0,1:T(8,128)(2,1)}), bf16[32,16,120]{2,0,1:T(8,128)(2,1)S(1)}, u32[]{:S(2)}, u32[]{:S(2)}) async-start(bf16[32,16,120]{2,0,1:T(8,128)(2,1)} %copy.47), calls=%async_computation | async-start | bytes 262144 | tf_op jit(solution)/shard_map/all_to_all | solution.py:77
  595.0 28.5 %copy-start.2 = (f32[120]{0:T(128)S(1)}, f32[120]{0:T(128)}, u32[]{:S(2)}) copy-start(f32[120]{0:T(128)} %param.25) | copy-start | bytes 1444
Sparse Core Ops, SparseCore 0:
  9.4 93.7 all-gather.6
  105.4 91.7 all-gather.8
  199.3 89.3 all-gather.10
  290.7 90.4 all-gather.12
  384.1 93.5 all-gather.14
  479.6 93.7 all-gather.16
where the time goes:
time: 633 us; the launch traced here: 632 us
  waiting for transfers between devices  479 us (76%)
  blocking collectives  48.9 us (8%)
  local copies, waits for them, and re-layouts  43.5 us (7%)
  matrix products  27.8 us (4%)
  between operations  15.1 us (2%)
  starting transfers between devices  8.71 us (1%)
    all_gather x4, waiting for transfers between devices, conv_layer(): whole = lax.all_gather(weight, ('section', 'dp'), axis=1, tiled=True)  297 us
    all_gather x1, waiting for transfers between devices, local(): lax.all_gather((project_weight, project_bias), 'tm', axis=1, tiled=True)  93.1 us
    all_gather x1, waiting for transfers between devices, local(): lax.all_gather(position_weight, ('section', 'dp'), axis=1, tiled=True)  72 us
    unnamed x1, blocking collectives  48.9 us
    all_gather x1, local copies, waits for them, and re-layouts, local(): lax.all_gather(position_weight, ('section', 'dp'), axis=1, tiled=True)  15.3 us
    all_to_all x1, waiting for transfers between devices, local(): lax.all_to_all(projected, 'tm', split_axis=1, concat_axis=0, tiled=True)  14.1 us
    while x120, local copies, waits for them, and re-layouts  12.8 us
  transfers between devices with their start and end apart: 9, of which 7 were waited for; matrix products, arithmetic and copies ran while one was open for 4% of the time, Pallas kernels for 0%

commit v1 on v0

v1 whole, which is shorter than its diff:
```python
import functools

import jax
import jax.numpy as jnp
from jax import lax
from jax.experimental import pallas as pl
from jax.experimental.pallas import tpu as pltpu
from jax.sharding import PartitionSpec as P

MESH = pl.DeviceIdType.MESH
CH = 512
GW = 120
EPS = 1e-05
HALO = 16
ROWS4 = 272
GROUPS_OF_TAPS = ((0, 1), (2, 3), (4, 5), (6, 7), (8, 9))
N_TAPS = 10


def norm(values):
    average = jnp.mean(values, axis=-1, keepdims=True)
    centred = values - average
    spread = jnp.mean(centred * centred, axis=-1, keepdims=True)
    return centred * lax.rsqrt(spread + EPS)


def gelu(values):
    return 0.5 * values * (1.0 + lax.erf(values * 0.7071067811865476))


def kernel(
    len_ref, frames_ref, w4_ref, w5_ref, w6_ref, w7_ref, gain_ref, nbias_ref,
    pw_ref, pb_ref, pos_ref, posb_ref, out_ref,
    wbuf, pbuf, halo, x4, x5, x6, x7, nbuf, hf, x16,
    local_sem, w_send, w_recv, p_send, p_recv, a_send, a_recv, h_send, h_recv,
):
    section = lax.axis_index("section")
    tm = lax.axis_index("tm")
    zl = lax.axis_index("dp")
    xi = section // 2
    core = lax.rem(section, 2)
    zh = tm // 4
    y = lax.rem(tm, 4)
    direction = 1 - 2 * core

    def at_x(by):
        return (lax.rem(xi + by + 4, 4) * 2 + core, tm, zl)

    def at_z(by):
        z = lax.rem(zh * 4 + zl + by + 16, 16)
        return (section, (z // 4) * 4 + y, lax.rem(z, 4))

    def at_line(by):
        return (section, tm, lax.rem(zl + by, 4))

    def at_zh(by):
        return (section, lax.rem(zh + by, 4) * 4 + y, zl)

    def at_y(by):
        return (section, zh * 4 + lax.rem(y + by, 4), zl)

    partner = (xi * 2 + 1 - core, tm, zl)
    before = (section, lax.rem(tm + 15, 16), zl)
    after = (section, lax.rem(tm + 1, 16), zl)

    greeted = [at_x(1), at_x(-1), at_z(1), at_z(-1), partner, before, after]
    greeted += [at_line(j) for j in (1, 2, 3)]
    greeted += [at_zh(j) for j in (1, 2, 3)]
    greeted += [at_y(j) for j in (1, 2, 3)]
    barrier = pltpu.get_barrier_semaphore()
    for other in greeted:
        pl.semaphore_signal(barrier, inc=1, device_id=other, device_id_type=MESH)
    pl.semaphore_wait(barrier, len(greeted))

    started = []

    def send(src, dst, send_sem, recv_sem, device):
        copy = pltpu.make_async_remote_copy(
            src_ref=src, dst_ref=dst, send_sem=send_sem, recv_sem=recv_sem,
            device_id=device, device_id_type=MESH,
        )
        copy.start()
        started.append(copy)
        return copy

    halo_copy = send(
        frames_ref.at[pl.ds(0, HALO)], halo, h_send, h_recv, before
    )

    shard_of = [(w4_ref, 0), (w4_ref, 1), (w4_ref, 2), (w5_ref, 0), (w5_ref, 1),
                (w5_ref, 2), (w6_ref, 0), (w6_ref, 1), (w7_ref, 0), (w7_ref, 1)]
    flows = [[None] * 7 for _ in range(N_TAPS)]
    own_copies = []

    def own_slot(k):
        return wbuf.at[k, xi, core, zl]

    def own_block(k):
        ref, tap = shard_of[k]
        return ref.at[tap]

    def first(k, by):
        return at_z(by) if k % 2 == 0 else at_x(by)

    def second(k, by):
        return at_x(by) if k % 2 == 0 else at_z(by)

    def stage0(k):
        mine = pltpu.make_async_copy(own_block(k), own_slot(k), local_sem.at[k])
        mine.start()
        own_copies.append(mine)
        for j, by in ((0, 1), (1, -1)):
            flows[k][j] = send(own_block(k), own_slot(k), w_send.at[k, j],
                               w_recv.at[k, j], first(k, by))

    def stage1(k):
        flows[k][0].wait_recv()
        flows[k][1].wait_recv()
        if k % 2 == 0:
            block = wbuf.at[k, xi, core, lax.rem(zl - direction + 4, 4)]
        else:
            block = wbuf.at[k, lax.rem(xi - direction + 4, 4), core, zl]
        flows[k][2] = send(block, block, w_send.at[k, 2], w_recv.at[k, 2],
                           first(k, direction))

    def column(k, by):
        if k % 2 == 0:
            return wbuf.at[k, lax.rem(xi + by + 4, 4), core]
        return wbuf.at[k, :, core, lax.rem(zl + by + 4, 4)]

    def stage2(k):
        flows[k][2].wait_recv()
        own_copies[k].wait()
        for j, by in ((3, 1), (4, -1)):
            flows[k][j] = send(column(k, 0), column(k, 0), w_send.at[k, j],
                               w_recv.at[k, j], second(k, by))

    def stage3(k):
        flows[k][3].wait_recv()
        flows[k][4].wait_recv()
        block = column(k, -direction)
        flows[k][5] = send(block, block, w_send.at[k, 5], w_recv.at[k, 5],
                           second(k, direction))

    def stage4(k):
        flows[k][5].wait_recv()
        block = wbuf.at[k, :, core]
        flows[k][6] = send(block, block, w_send.at[k, 6], w_recv.at[k, 6], partner)

    def stage5(k):
        flows[k][6].wait_recv()

    stages = (stage0, stage1, stage2, stage3, stage4, stage5)

    pos_flows = [None] * 7
    pos_slot = pbuf.at[lax.rem(xi, 2), core, zl, xi // 2]

    def pos0():
        mine = pltpu.make_async_copy(pos_ref, pos_slot, local_sem.at[N_TAPS])
        mine.start()
        own_copies.append(mine)
        for j in range(3):
            pos_flows[j] = send(pos_ref, pos_slot, p_send.at[j], p_recv.at[j],
                                at_line(j + 1))

    def pos_column(by):
        x = lax.rem(xi + by + 4, 4)
        return pbuf.at[lax.rem(x, 2), core, :, x // 2]

    def pos1():
        for j in range(3):
            pos_flows[j].wait_recv()
        own_copies[-1].wait()
        for j, by in ((3, 1), (4, -1)):
            pos_flows[j] = send(pos_column(0), pos_column(0), p_send.at[j],
                                p_recv.at[j], at_x(by))

    def pos2():
        pos_flows[3].wait_recv()
        pos_flows[4].wait_recv()
        block = pos_column(-direction)
        pos_flows[5] = send(block, block, p_send.at[5], p_recv.at[5], at_x(direction))

    def pos3():
        pos_flows[5].wait_recv()
        block = pbuf.at[:, core]
        pos_flows[6] = send(block, block, p_send.at[6], p_recv.at[6], partner)

    def pos4():
        pos_flows[6].wait_recv()

    length = len_ref[0]

    def masked(block, base):
        rows = block.shape[0]
        index = base + lax.broadcasted_iota(jnp.int32, (rows, CH), 0)
        kept = jnp.where(index * 20 < length, block.astype(jnp.float32), 0.0)
        return kept

    def prepare():
        put(x4, 0, masked(frames_ref[...], tm * CH))
        put(x4, CH + HALO, jnp.zeros((32, CH), jnp.float32))
        hf[...] = jnp.zeros(hf.shape, jnp.float32)

    def prepare_halo():
        halo_copy.wait_recv()
        put(x4, CH, masked(halo[...], tm * CH + CH))

    def conv(x_ref, k, taps, rows):
        total = None
        for tap in range(taps):
            picked = jnp.concatenate(
                [x_ref[b, pl.ds(tap, rows, stride=2), :] for b in range(4)], axis=1
            ).astype(jnp.bfloat16)
            weight = wbuf[k + tap].reshape(CH, CH)
            part = jnp.dot(picked, weight, preferred_element_type=jnp.float32)
            total = part if total is None else total + part
        return gelu(norm(total)).astype(jnp.bfloat16).astype(jnp.float32)

    def put(x_ref, start, value):
        for b in range(4):
            x_ref[b, pl.ds(start, value.shape[0]), :] = value[:, b * 128 : b * 128 + 128]

    def layer4():
        prepare_halo()
        put(x5, 0, conv(x4, 0, 3, ROWS4))

    def layer5():
        put(x6, 0, conv(x5, 3, 3, 128))

    def layer6():
        put(x7, 0, conv(x6, 6, 2, 64))

    zh_flows = []

    def layer7():
        last = conv(x7, 8, 2, 32)
        normed = norm(last) * gain_ref[...] + nbias_ref[...]
        nbuf[tm] = normed.astype(jnp.bfloat16)
        block = nbuf.at[tm]
        for j in range(3):
            zh_flows.append(send(block, block, a_send.at[j], a_recv.at[j], at_zh(j + 1)))

    compute_after = {1: layer4, 2: layer5, 3: layer6, 4: layer7}
    n_groups = len(GROUPS_OF_TAPS)
    pos_at = {4: pos0, 7: pos1, 9: pos2}
    for step in range(n_groups + 5):
        for stage in range(5, -1, -1):
            group = step - stage
            if 0 <= group < n_groups:
                for k in GROUPS_OF_TAPS[group]:
                    stages[stage](k)
        if step in pos_at:
            pos_at[step]()
        if step == 1:
            prepare()
        done = step - 5
        if done in compute_after:
            compute_after[done]()

    y_flows = []
    for j in range(4):
        source = lax.rem(zh - j + 4, 4) * 4 + y
        if j:
            zh_flows[j - 1].wait_recv()
        block = nbuf.at[source]
        for by in (1, 2, 3):
            slot = 3 + j * 3 + by - 1
            y_flows.append(send(block, block, a_send.at[slot], a_recv.at[slot], at_y(by)))
    pos3()
    for copy in y_flows:
        copy.wait_recv()

    gathered = nbuf[...].reshape(CH, CH)
    hidden = jnp.dot(gathered, pw_ref[...], preferred_element_type=jnp.float32)
    hidden = (hidden + pb_ref[...].astype(jnp.float32)).astype(jnp.bfloat16)
    frame = lax.broadcasted_iota(jnp.int32, (CH, GW), 0)
    hidden = jnp.where(frame * 320 < length, hidden.astype(jnp.float32), 0.0)
    hf[pl.ds(64, CH), pl.ds(0, GW)] = hidden
    for tap in range(16):
        x16[:, pl.ds(tap * 128, 128)] = hf[pl.ds(tap, 624), :].astype(jnp.bfloat16)
    pos4()
    total = None
    for m in range(4):
        weight = jnp.concatenate(
            [pbuf[m // 2, m % 2, q].reshape(256, 512) for q in range(4)], axis=1
        )
        part = lax.dot_general(
            x16[pl.ds(16 * m, 576), :], weight, (((1,), (1,)), ((), ())),
            preferred_element_type=jnp.float32,
        )
        total = part if total is None else total + part
    conv_out = total[:CH, :128] + total[64:, 128:]
    position = gelu(conv_out[:, :GW] + posb_ref[...])
    encoded = hf[pl.ds(64, CH), pl.ds(0, GW)] + position
    out_ref[...] = encoded.T.astype(jnp.bfloat16)
    for copy in started:
        copy.wait_send()


def local(
    frames, lengths, fourth_conv, fifth_conv, sixth_conv, seventh_conv,
    norm_gain, norm_bias, project_weight, project_bias, position_weight, position_bias,
):
    taps = position_weight.reshape(4, GW, GW).transpose(1, 0, 2)
    taps = jnp.pad(taps, ((0, 8), (0, 0), (0, 8))).reshape(128, 512)
    vmem = pl.BlockSpec(memory_space=pltpu.VMEM)
    dma = pltpu.SemaphoreType.DMA
    out = pl.pallas_call(
        kernel,
        out_shape=jax.ShapeDtypeStruct((GW, CH), jnp.bfloat16),
        in_specs=[pl.BlockSpec(memory_space=pltpu.SMEM)] + [vmem] * 11,
        out_specs=vmem,
        scratch_shapes=[
            pltpu.VMEM((N_TAPS, 4, 2, 4, 16, CH), jnp.bfloat16),
            pltpu.VMEM((2, 2, 4, 2, 128, 512), jnp.bfloat16),
            pltpu.VMEM((HALO, CH), jnp.bfloat16),
            pltpu.VMEM((4, CH + HALO + 32, 128), jnp.float32),
            pltpu.VMEM((4, ROWS4, 128), jnp.float32),
            pltpu.VMEM((4, 128, 128), jnp.float32),
            pltpu.VMEM((4, 64, 128), jnp.float32),
            pltpu.VMEM((16, 32, CH), jnp.bfloat16),
            pltpu.VMEM((640, 128), jnp.float32),
            pltpu.VMEM((624, 2048), jnp.bfloat16),
            dma((N_TAPS + 1,)),
            dma((N_TAPS, 7)),
            dma((N_TAPS, 7)),
            dma((7,)),
            dma((7,)),
            dma((15,)),
            dma((15,)),
            dma,
            dma,
        ],
        compiler_params=pltpu.CompilerParams(
            collective_id=0, has_side_effects=True, vmem_limit_bytes=60 * 1024 * 1024
        ),
    )(
        lengths, frames[0], fourth_conv, fifth_conv, sixth_conv, seventh_conv,
        norm_gain.reshape(1, CH), norm_bias.reshape(1, CH),
        project_weight, project_bias, taps, position_bias.reshape(1, GW),
    )
    return out[None]


def solution(mesh):
    in_specs = (
        P(("section", "dp"), "tm", None),
        P(("section", "dp")),
        P(None, ("section", "dp"), None),
        P(None, ("section", "dp"), None),
        P(None, ("section", "dp"), None),
        P(None, ("section", "dp"), None),
        P(),
        P(),
        P(None, "tm"),
        P(None, "tm"),
        P("tm", ("section", "dp"), None),
        P("tm"),
    )
    out_specs = P(("section", "dp"), "tm", None)
    return jax.shard_map(local, mesh=mesh, in_specs=in_specs, out_specs=out_specs, check_vma=False)
```

time: 633 us -> 89.9 us (0.14)
  waiting for transfers between devices: 479 us -> 0 us
  Pallas kernels: 0 us -> 84.6 us
  blocking collectives: 48.9 us -> 0 us
  local copies, waits for them, and re-layouts: 43.5 us -> 4.45 us
  matrix products: 27.8 us -> 0 us
  between operations: 15.1 us -> 0.69 us
  starting transfers between devices: 8.71 us -> 0 us
    all_gather x6 -> x0, waiting for transfers between devices: 462 us -> none  [the longest x4 297 us: conv_layer(): whole = lax.all_gather(weight, ('section', 'dp'), axis=1, tiled=True)]
    pallas_call x0 -> x1, Pallas kernels: none -> 84.6 us  [local(): pl.pallas_call(kernel, out_shape=jax.ShapeDtypeStruct((GW, CH), jnp.bfloa...]
    unnamed x1 -> x0, blocking collectives: 48.9 us -> none
    dot_general x19 -> x0, matrix products: 27.8 us -> none  [the longest x8 12.4 us: one_block(): lax.dot_general(tap_weights, window, (((0, 2), (1, 2)), ((), ())), prefer...]
    all_gather x1 -> x0, local copies, waits for them, and re-layouts: 15.3 us -> none  [local(): lax.all_gather(position_weight, ('section', 'dp'), axis=1, tiled=True)]
    all_to_all x1 -> x0, waiting for transfers between devices: 14.1 us -> none  [local(): lax.all_to_all(projected, 'tm', split_axis=1, concat_axis=0, tiled=True)]
    while x121 -> x0, local copies, waits for them, and re-layouts: 12.9 us -> none
    unnamed x12 -> x5, local copies, waits for them, and re-layouts: 10.3 us -> 3.23 us
  transfers between devices with their start and end apart: 9 -> 0, of which waited for: 7 -> 0; matrix products, arithmetic and copies ran while one was open for 4% -> 0% of each run, Pallas kernels for 0% -> 0%
where the time goes in v1:
time: 89.9 us; the launch traced here: 89.7 us
  Pallas kernels  84.6 us (94%)
  local copies, waits for them, and re-layouts  4.45 us (5%)
    pallas_call x1, Pallas kernels, local(): pl.pallas_call(kernel, out_shape=jax.ShapeDtypeStruct((GW, CH), jnp.bfloa...  84.6 us
    unnamed x5, local copies, waits for them, and re-layouts  3.23 us

profile of v1, /device:TPU:7, one launch (start us, length us, event | category | flops | bytes accessed | tf_op | source)
XLA Modules:
  0.0 89.7 jit_solution(5907896809985816001)
XLA Ops:
  0.7 1.1 %reshape.17 = bf16[4,120,120]{2,1,0:T(8,128)(2,1)S(1)} reshape(bf16[1,4,14400]{2,1,0:T(4,128)(2,1)} %param.22) | data formatting | bytes 230400 | tf_op jit(solution)/shard_map/reshape | solution.py:305
  1.8 0.1 pad.4
  1.9 0.0 copy-start
  1.9 0.7 copy.18
  2.6 0.2 copy-done
  2.8 0.8 copy.14.pw_ref
  3.6 84.6 %shard_map.118 = bf16[120,512]{1,0:T(8,128)(2,1)} custom-call(s32[1]{0:T(128)S(6)} %copy.21.len_ref, bf16[512,512]{1,0:T(8,128)(2,1)} %bitcast.13, bf16[3,16,512]{2,1,0:T(8,128)(2,1)} %w4_ref.1, bf16[3,16,512]{2,1,0:T(8,128)(2,1)} %w5_ref.1, bf16[2,16,512]{2,1,0:T(8,128)(2,1)} %w6_ref.1, bf16[2,16,512]{2,1,0:T(8,128)(2,1)} %w7_ref.1, f32[1,512]{1,0:T(1,128)} %bitcast.17, ...), custom_call_target="tpu_custom_call" | custom-call | tf_op jit(solution)/shard_map/pallas_call | solution.py:309
  88.1 1.6 %copy.22 = bf16[1,120,512]{2,1,0:T(8,128)(2,1)} copy(bf16[1,120,512]{2,1,0:T(8,128)(2,1)} %bitcast.15) | data formatting | bytes 245760
  (1 shorter events, 0.0 us)
Async XLA Ops:
  1.9 0.9 %copy-start = (bf16[512,120]{0,1:T(8,128)(2,1)S(1)}, bf16[512,120]{0,1:T(8,128)(2,1)}, u32[]{:S(2)}) copy-start(bf16[512,120]{0,1:T(8,128)(2,1)} %param.20) | copy-start | bytes 368644

commit v2 on v1

v2 whole, which is shorter than its diff:
```python
import jax
import jax.numpy as jnp
from jax import lax
from jax.experimental import pallas as pl
from jax.experimental.pallas import tpu as pltpu
from jax.sharding import PartitionSpec as P

MESH = pl.DeviceIdType.MESH
CH = 512
GW = 120
EPS = 1e-05
HALO = 16
ROWS4 = 272
N_TAPS = 10
WINDOW = 4
LAG4 = 2
LAG5 = 4


def norm(values):
    average = jnp.mean(values, axis=-1, keepdims=True)
    centred = values - average
    spread = jnp.mean(centred * centred, axis=-1, keepdims=True)
    return centred * lax.rsqrt(spread + EPS)


def gelu(values):
    return 0.5 * values * (1.0 + lax.erf(values * 0.7071067811865476))


def kernel(
    len_ref, frames_ref, w4_ref, w5_ref, w6_ref, w7_ref, gain_ref, nbias_ref,
    pw_ref, pb_ref, pos_ref, posb_ref, out_ref,
    wbuf, pbuf, fbuf, qbuf, pwbuf, halo, x4, x5, x6, x7, nbuf, hf, x16, relay32,
    local_sem, w_send, w_recv, p_send, p_recv, a_send, a_recv, h_send, h_recv, rounds,
):
    section = lax.axis_index("section")
    tm = lax.axis_index("tm")
    zl = lax.axis_index("dp")
    xi = section // 2
    core = lax.rem(section, 2)
    zh = tm // 4
    y = lax.rem(tm, 4)
    direction = 1 - 2 * core

    def at_x(by):
        return (lax.rem(xi + by + 4, 4) * 2 + core, tm, zl)

    def at_z(by):
        z = lax.rem(zh * 4 + zl + by + 16, 16)
        return (section, (z // 4) * 4 + y, lax.rem(z, 4))

    def at_line(by):
        return (section, tm, lax.rem(zl + by, 4))

    def at_zh(by):
        return (section, lax.rem(zh + by, 4) * 4 + y, zl)

    def at_y(by):
        return (section, zh * 4 + lax.rem(y + by + 4, 4), zl)

    partner = (xi * 2 + 1 - core, tm, zl)
    before = (section, lax.rem(tm + 15, 16), zl)

    def signal(sem, others):
        for other in others:
            pl.semaphore_signal(sem, inc=1, device_id=other, device_id_type=MESH)

    barrier = pltpu.get_barrier_semaphore()
    near = [partner, at_x(1), at_x(-1), at_z(1), at_z(-1), at_y(1), at_y(-1)]
    signal(barrier, near)

    fetches = []

    def fetch(src, dst):
        copy = pltpu.make_async_copy(src, dst, local_sem.at[len(fetches)])
        copy.start()
        fetches.append(copy)

    fetch(w4_ref, wbuf.at[pl.ds(0, 3), xi, core, zl])
    fetch(w5_ref, wbuf.at[pl.ds(3, 3), xi, core, zl])
    fetch(w6_ref, wbuf.at[pl.ds(6, 2), xi, core, zl])
    fetch(w7_ref, wbuf.at[pl.ds(8, 2), xi, core, zl])
    fetch(frames_ref, fbuf)
    fetch(pos_ref, qbuf)
    fetch(pw_ref, pwbuf)

    started = []

    def send(src, dst, send_sem, recv_sem, device):
        copy = pltpu.make_async_remote_copy(
            src_ref=src, dst_ref=dst, send_sem=send_sem, recv_sem=recv_sem,
            device_id=device, device_id_type=MESH,
        )
        copy.start()
        started.append(copy)
        return copy

    flows = [[None] * 7 for _ in range(N_TAPS)]

    def own(k):
        return wbuf.at[k, xi, core, zl]

    def first(k, by):
        return at_z(by) if k % 2 == 0 else at_x(by)

    def second(k, by):
        return at_x(by) if k % 2 == 0 else at_z(by)

    def flow(k, j, block, device):
        flows[k][j] = send(block, block, w_send.at[k, j], w_recv.at[k, j], device)

    def stage0(k):
        flow(k, 0, own(k), first(k, 1))
        flow(k, 1, own(k), first(k, -1))

    def stage1(k):
        flows[k][0].wait_recv()
        flows[k][1].wait_recv()
        if k % 2 == 0:
            block = wbuf.at[k, xi, core, lax.rem(zl - direction + 4, 4)]
        else:
            block = wbuf.at[k, lax.rem(xi - direction + 4, 4), core, zl]
        flow(k, 2, block, first(k, direction))

    def column(k, by):
        if k % 2 == 0:
            return wbuf.at[k, lax.rem(xi + by + 4, 4), core]
        return wbuf.at[k, :, core, lax.rem(zl + by + 4, 4)]

    def stage2(k):
        flows[k][2].wait_recv()
        flow(k, 3, column(k, 0), second(k, 1))
        flow(k, 4, column(k, 0), second(k, -1))

    def stage3(k):
        flows[k][3].wait_recv()
        flows[k][4].wait_recv()
        flow(k, 5, column(k, -direction), second(k, direction))

    def stage4(k):
        flows[k][5].wait_recv()
        flow(k, 6, wbuf.at[k, :, core], partner)

    def stage5(k):
        flows[k][6].wait_recv()

    pos_flows = {}

    def pos_block(x, z):
        return pbuf.at[lax.rem(x, 2), core, z, x // 2, pl.ds(0, GW)]

    def pos_send(name, block, device):
        j = len(pos_flows)
        pos_flows[name] = send(block, block, p_send.at[j], p_recv.at[j], device)

    def arrange_pos():
        values = qbuf[...].astype(jnp.float32)
        values = jnp.concatenate([values, jnp.zeros((4, 64), jnp.float32)], axis=1)
        for o in range(GW):
            relay32[pl.ds(o, 4, stride=128), :] = values[:, o * GW : o * GW + 128]
        for tap in range(4):
            pbuf[lax.rem(xi, 2), core, zl, xi // 2, :, pl.ds(tap * 128, 128)] = (
                relay32[pl.ds(tap * 128, 128), :].astype(jnp.bfloat16)
            )

    def pos_start():
        for j in (1, 2, 3):
            pos_send(("z", j), pos_block(xi, zl), at_line(j))
        pos_send(("x", 0, 1), pos_block(xi, zl), at_x(1))
        pos_send(("x", 0, -1), pos_block(xi, zl), at_x(-1))

    def pos_forward(j):
        pos_flows["z", j].wait_recv()
        block = pos_block(xi, lax.rem(zl - j + 4, 4))
        pos_send(("x", j, 1), block, at_x(1))
        pos_send(("x", j, -1), block, at_x(-1))

    def pos_relay(j):
        pos_flows["x", j, 1].wait_recv()
        pos_flows["x", j, -1].wait_recv()
        block = pos_block(lax.rem(xi - direction + 4, 4), lax.rem(zl - j + 4, 4))
        pos_send(("r", j), block, at_x(direction))

    def pos_swap(j):
        pos_flows["r", j].wait_recv()
        z = lax.rem(zl - j + 4, 4)
        block = pbuf.at[:, core, z, :, pl.ds(0, GW)]
        pos_send(("p", j), block, partner)

    length = len_ref[0]

    def masked(block, base):
        rows = block.shape[0]
        index = base + lax.broadcasted_iota(jnp.int32, (rows, CH), 0)
        return jnp.where(index * 20 < length, block.astype(jnp.float32), 0.0)

    def put(x_ref, start, value):
        for b in range(4):
            x_ref[b, pl.ds(start, value.shape[0]), :] = value[:, b * 128 : b * 128 + 128]

    def conv(x_ref, k, taps, rows):
        total = None
        for tap in range(taps):
            picked = jnp.concatenate(
                [x_ref[b, pl.ds(tap, rows, stride=2), :] for b in range(4)], axis=1
            ).astype(jnp.bfloat16)
            weight = wbuf[k + tap].reshape(CH, CH)
            part = jnp.dot(picked, weight, preferred_element_type=jnp.float32)
            total = part if total is None else total + part
        return gelu(norm(total)).astype(jnp.bfloat16).astype(jnp.float32)

    hf[...] = jnp.zeros(hf.shape, jnp.float32)
    put(x4, CH + HALO, jnp.zeros((32, CH), jnp.float32))
    for j in range(4):
        fetches[j].wait()
    pl.semaphore_wait(barrier, len(near))

    for k in range(N_TAPS):
        stage0(k)
    signal(rounds.at[0], [at_z(1), at_z(-1), at_y(1), at_y(-1)])
    fetches[4].wait()
    put(x4, 0, masked(fbuf[...], tm * CH))
    for k in range(N_TAPS):
        stage1(k)
        if k == 4:
            pl.semaphore_wait(rounds.at[0], 4)
            signal(rounds.at[1], [at_z(2), at_z(-2)])
    for k in range(WINDOW):
        stage2(k)
    pl.semaphore_wait(rounds.at[1], 2)
    signal(rounds.at[2], [at_z(4), at_z(-4)])
    fetches[5].wait()
    arrange_pos()
    pl.semaphore_wait(rounds.at[2], 2)
    halo_copy = send(frames_ref.at[pl.ds(0, HALO)], halo, h_send, h_recv, before)

    for step in range(N_TAPS + LAG5):
        if step < N_TAPS:
            stage3(step)
        if step + WINDOW < N_TAPS:
            stage2(step + WINDOW)
        if step == N_TAPS - 1:
            pos_start()
        if 0 <= step - LAG4 < N_TAPS:
            stage4(step - LAG4)
        done = step - LAG5
        if done >= 0:
            stage5(done)
            if done == 2:
                halo_copy.wait_recv()
                put(x4, CH, masked(halo[...], tm * CH + CH))
                put(x5, 0, conv(x4, 0, 3, ROWS4))
            if done == 5:
                put(x6, 0, conv(x5, 3, 3, 128))
            if done == 7:
                put(x7, 0, conv(x6, 6, 2, 64))
    last = conv(x7, 8, 2, 32)
    normed = norm(last) * gain_ref[...] + nbias_ref[...]
    nbuf[tm] = normed.astype(jnp.bfloat16)

    act_flows = {}

    def act_send(name, block, device):
        j = len(act_flows)
        act_flows[name] = send(block, block, a_send.at[j], a_recv.at[j], device)

    for j in (1, 3, 2):
        act_send(("z", j), nbuf.at[tm], at_zh(j))
    for by in (1, 2, 3):
        act_send(("y", 0, by), nbuf.at[tm], at_y(by))
    pos_relay(0)
    for j in (1, 2, 3):
        pos_forward(j)
    for j in (1, 3, 2):
        act_flows["z", j].wait_recv()
        block = nbuf.at[lax.rem(zh - j + 4, 4) * 4 + y]
        for by in (1, 2, 3):
            act_send(("y", j, by), block, at_y(by))
    pos_swap(0)
    for j in (1, 2, 3):
        pos_relay(j)
    fetches[6].wait()
    for j in range(4):
        for by in (1, 2, 3):
            act_flows["y", j, by].wait_recv()

    gathered = nbuf[...].reshape(CH, CH)
    hidden = lax.dot_general(
        gathered, pwbuf[...], (((1,), (1,)), ((), ())), preferred_element_type=jnp.float32
    )
    hidden = (hidden + pb_ref[...].astype(jnp.float32)).astype(jnp.bfloat16)
    frame = lax.broadcasted_iota(jnp.int32, (CH, GW), 0)
    hidden = jnp.where(frame * 320 < length, hidden.astype(jnp.float32), 0.0)
    hf[pl.ds(64, CH), pl.ds(0, GW)] = hidden
    for j in (1, 2, 3):
        pos_swap(j)
    for tap in range(16):
        x16[:, pl.ds(tap * 128, 128)] = hf[pl.ds(tap, 624), :].astype(jnp.bfloat16)
    for j in range(4):
        pos_flows["p", j].wait_recv()
    total = None
    for m in range(4):
        weight = jnp.concatenate(
            [pbuf[m // 2, m % 2, q].reshape(256, 512) for q in range(4)], axis=1
        )
        part = lax.dot_general(
            x16[pl.ds(16 * m, 576), :], weight, (((1,), (1,)), ((), ())),
            preferred_element_type=jnp.float32,
        )
        total = part if total is None else total + part
    conv_out = total[:CH, :128] + total[64:, 128:]
    position = gelu(conv_out[:, :GW] + posb_ref[...])
    encoded = hf[pl.ds(64, CH), pl.ds(0, GW)] + position
    out_ref[...] = encoded.T.astype(jnp.bfloat16)
    for copy in started:
        copy.wait_send()


def local(
    frames, lengths, fourth_conv, fifth_conv, sixth_conv, seventh_conv,
    norm_gain, norm_bias, project_weight, project_bias, position_weight, position_bias,
):
    vmem = pl.BlockSpec(memory_space=pltpu.VMEM)
    hbm = pl.BlockSpec(memory_space=pl.ANY)
    smem = pl.BlockSpec(memory_space=pltpu.SMEM)
    dma = pltpu.SemaphoreType.DMA
    out = pl.pallas_call(
        kernel,
        out_shape=jax.ShapeDtypeStruct((GW, CH), jnp.bfloat16),
        in_specs=[smem, hbm, hbm, hbm, hbm, hbm, vmem, vmem, hbm, vmem, hbm, vmem],
        out_specs=vmem,
        scratch_shapes=[
            pltpu.VMEM((N_TAPS, 4, 2, 4, 16, CH), jnp.bfloat16),
            pltpu.VMEM((2, 2, 4, 2, 128, 512), jnp.bfloat16),
            pltpu.VMEM((CH, CH), jnp.bfloat16),
            pltpu.VMEM((4, GW * GW), jnp.bfloat16),
            pltpu.VMEM((GW, CH), jnp.bfloat16),
            pltpu.VMEM((HALO, CH), jnp.bfloat16),
            pltpu.VMEM((4, CH + HALO + 32, 128), jnp.float32),
            pltpu.VMEM((4, ROWS4, 128), jnp.float32),
            pltpu.VMEM((4, 128, 128), jnp.float32),
            pltpu.VMEM((4, 64, 128), jnp.float32),
            pltpu.VMEM((16, 32, CH), jnp.bfloat16),
            pltpu.VMEM((640, 128), jnp.float32),
            pltpu.VMEM((624, 2048), jnp.bfloat16),
            pltpu.VMEM((512, 128), jnp.float32),
            dma((7,)),
            dma((N_TAPS, 7)),
            dma((N_TAPS, 7)),
            dma((19,)),
            dma((19,)),
            dma((15,)),
            dma((15,)),
            dma,
            dma,
            pltpu.SemaphoreType.REGULAR((3,)),
        ],
        compiler_params=pltpu.CompilerParams(
            collective_id=0, has_side_effects=True, vmem_limit_bytes=60 * 1024 * 1024
        ),
    )(
        lengths, frames[0], fourth_conv, fifth_conv, sixth_conv, seventh_conv,
        norm_gain.reshape(1, CH), norm_bias.reshape(1, CH),
        project_weight.T, project_bias, position_weight[0], position_bias.reshape(1, GW),
    )
    return out[None]


def solution(mesh):
    in_specs = (
        P(("section", "dp"), "tm", None),
        P(("section", "dp")),
        P(None, ("section", "dp"), None),
        P(None, ("section", "dp"), None),
        P(None, ("section", "dp"), None),
        P(None, ("section", "dp"), None),
        P(),
        P(),
        P(None, "tm"),
        P(None, "tm"),
        P("tm", ("section", "dp"), None),
        P("tm"),
    )
    out_specs = P(("section", "dp"), "tm", None)
    return jax.shard_map(local, mesh=mesh, in_specs=in_specs, out_specs=out_specs, check_vma=False)
```

time: 89.9 us -> 73.3 us (0.82)
  the two profiles are of different devices: /device:TPU:7 before, /device:TPU:97 now
where the time goes in v2:
time: 73.3 us; the launch traced here: 73.1 us
  Pallas kernels  70.9 us (97%)
  local copies, waits for them, and re-layouts  1.56 us (2%)
    pallas_call x1, Pallas kernels, local(): pl.pallas_call(kernel, out_shape=jax.ShapeDtypeStruct((GW, CH), jnp.bfloa...  70.9 us
    unnamed x1, local copies, waits for them, and re-layouts  1.56 us

profile of v2, /device:TPU:97, one launch (start us, length us, event | category | flops | bytes accessed | tf_op | source)
XLA Modules:
  0.0 73.1 jit_solution(12461963855548251967)
XLA Ops:
  0.7 70.9 %shard_map.118 = bf16[120,512]{1,0:T(8,128)(2,1)} custom-call(s32[1]{0:T(128)S(6)} %copy.14.len_ref, bf16[512,512]{1,0:T(8,128)(2,1)} %bitcast.7, bf16[3,16,512]{2,1,0:T(8,128)(2,1)} %w4_ref.1, bf16[3,16,512]{2,1,0:T(8,128)(2,1)} %w5_ref.1, bf16[2,16,512]{2,1,0:T(8,128)(2,1)} %w6_ref.1, bf16[2,16,512]{2,1,0:T(8,128)(2,1)} %w7_ref.1, f32[1,512]{1,0:T(1,128)} %bitcast.11, ...), custom_call_target="tpu_custom_call" | custom-call | tf_op jit(solution)/shard_map/pallas_call | solution.py:328
  71.5 1.6 %copy.15 = bf16[1,120,512]{2,1,0:T(8,128)(2,1)} copy(bf16[1,120,512]{2,1,0:T(8,128)(2,1)} %bitcast.8) | data formatting | bytes 245760

commit v3 on v2

--- a/solution.py
+++ b/solution.py
@@ -12,9 +12,7 @@
 HALO = 16
 ROWS4 = 272
 N_TAPS = 10
-WINDOW = 4
-LAG4 = 2
-LAG5 = 4
+PLAIN = 6
 
 
 def norm(values):
@@ -31,7 +29,7 @@
 def kernel(
     len_ref, frames_ref, w4_ref, w5_ref, w6_ref, w7_ref, gain_ref, nbias_ref,
     pw_ref, pb_ref, pos_ref, posb_ref, out_ref,
-    wbuf, pbuf, fbuf, qbuf, pwbuf, halo, x4, x5, x6, x7, nbuf, hf, x16, relay32,
+    wbuf, stage, pbuf, fbuf, qbuf, pwbuf, bbuf, halo, x4, x5, x6, x7, nbuf, sbuf, hbuf, hf, x16, relay32,
     local_sem, w_send, w_recv, p_send, p_recv, a_send, a_recv, h_send, h_recv, rounds,
 ):
     section = lax.axis_index("section")
@@ -66,9 +64,14 @@
         for other in others:
             pl.semaphore_signal(sem, inc=1, device_id=other, device_id_type=MESH)
 
+    def at_plane(dx, dz):
+        by = dz * direction if dz == 2 else dz
+        z = lax.rem(zh * 4 + zl + by + 16, 16)
+        return (lax.rem(xi + dx + 4, 4) * 2 + core, (z // 4) * 4 + y, lax.rem(z, 4))
+
     barrier = pltpu.get_barrier_semaphore()
-    near = [partner, at_x(1), at_x(-1), at_z(1), at_z(-1), at_y(1), at_y(-1)]
-    signal(barrier, near)
+    beside = [at_x(1), at_x(-1), at_z(1), at_z(-1), at_y(1), at_y(-1)]
+    signal(barrier, beside + [partner])
 
     fetches = []
 
@@ -79,11 +82,11 @@
 
     fetch(w4_ref, wbuf.at[pl.ds(0, 3), xi, core, zl])
     fetch(w5_ref, wbuf.at[pl.ds(3, 3), xi, core, zl])
-    fetch(w6_ref, wbuf.at[pl.ds(6, 2), xi, core, zl])
-    fetch(w7_ref, wbuf.at[pl.ds(8, 2), xi, core, zl])
+    fetch(w6_ref, stage.at[pl.ds(0, 2)])
+    fetch(w7_ref, stage.at[pl.ds(2, 2)])
     fetch(frames_ref, fbuf)
     fetch(pos_ref, qbuf)
-    fetch(pw_ref, pwbuf)
+    fetch(pw_ref, pwbuf.at[y])
 
     started = []
 
@@ -96,54 +99,67 @@
         started.append(copy)
         return copy
 
-    flows = [[None] * 7 for _ in range(N_TAPS)]
+    flows = {}
+
+    def flow(name, block, device):
+        j = len(flows)
+        flows[name] = send(block, block, w_send.at[j], w_recv.at[j], device)
 
     def own(k):
         return wbuf.at[k, xi, core, zl]
 
-    def first(k, by):
-        return at_z(by) if k % 2 == 0 else at_x(by)
-
-    def second(k, by):
-        return at_x(by) if k % 2 == 0 else at_z(by)
-
-    def flow(k, j, block, device):
-        flows[k][j] = send(block, block, w_send.at[k, j], w_recv.at[k, j], device)
-
-    def stage0(k):
-        flow(k, 0, own(k), first(k, 1))
-        flow(k, 1, own(k), first(k, -1))
-
-    def stage1(k):
-        flows[k][0].wait_recv()
-        flows[k][1].wait_recv()
-        if k % 2 == 0:
-            block = wbuf.at[k, xi, core, lax.rem(zl - direction + 4, 4)]
-        else:
-            block = wbuf.at[k, lax.rem(xi - direction + 4, 4), core, zl]
-        flow(k, 2, block, first(k, direction))
-
-    def column(k, by):
+    def stage0(k, by):
+        device = at_plane(0, by) if k % 2 == 0 else at_plane(by, 0)
+        flow(("a", k, by), own(k), device)
+
+    def line(k, by):
         if k % 2 == 0:
             return wbuf.at[k, lax.rem(xi + by + 4, 4), core]
         return wbuf.at[k, :, core, lax.rem(zl + by + 4, 4)]
 
+    def second(k, by):
+        return at_x(by) if k % 2 == 0 else at_z(by)
+
+    def stage1(k):
+        for by in (1, -1, 2):
+            flows["a", k, by].wait_recv()
+        flow(("b", k, 1), line(k, 0), second(k, 1))
+        flow(("b", k, -1), line(k, 0), second(k, -1))
+
+    def pass_on(k):
+        flows["b", k, 1].wait_recv()
+        flows["b", k, -1].wait_recv()
+        flow(("b", k, 2), line(k, -direction), second(k, direction))
+
     def stage2(k):
-        flows[k][2].wait_recv()
-        flow(k, 3, column(k, 0), second(k, 1))
-        flow(k, 4, column(k, 0), second(k, -1))
-
-    def stage3(k):
-        flows[k][3].wait_recv()
-        flows[k][4].wait_recv()
-        flow(k, 5, column(k, -direction), second(k, direction))
-
-    def stage4(k):
-        flows[k][5].wait_recv()
-        flow(k, 6, wbuf.at[k, :, core], partner)
-
-    def stage5(k):
-        flows[k][6].wait_recv()
+        flows["b", k, 2].wait_recv()
+        flow(("p", k), wbuf.at[k, :, core], partner)
+
+    shared = PLAIN + y
+
+    def share0(dx, dz):
+        j = len(flows)
+        flows["s", dx, dz] = send(
+            stage.at[y], wbuf.at[shared, xi, core, zl], w_send.at[j], w_recv.at[j],
+            at_plane(dx, dz),
+        )
+
+    def lend(by):
+        flow(("w", by), pwbuf.at[y], at_y(by))
+        flow(("c", by), bbuf.at[y], at_y(by))
+
+    def share1(dx):
+        for dz in (0, 1, -1, 2):
+            if (dx, dz) != (0, 0):
+                flows["s", dx, dz].wait_recv()
+        block = wbuf.at[shared, lax.rem(xi - dx + 4, 4), core]
+        for by in (1, 3, 2):
+            flow(("y", dx, by), block, at_y(by))
+
+    def share2(by):
+        for dx in (0, 1, -1, 2):
+            flows["y", dx, by].wait_recv()
+        flow(("q", by), wbuf.at[PLAIN + lax.rem(y - by + 4, 4), :, core], partner)
 
     pos_flows = {}
 
@@ -210,93 +226,132 @@
             total = part if total is None else total + part
         return gelu(norm(total)).astype(jnp.bfloat16).astype(jnp.float32)
 
+    bias = jnp.concatenate(
+        [pb_ref[...].astype(jnp.float32), jnp.zeros((1, 128 - GW), jnp.float32)], axis=1
+    )
+    bbuf[y] = jnp.broadcast_to(bias, (16, 128)).astype(jnp.bfloat16)
     hf[...] = jnp.zeros(hf.shape, jnp.float32)
     put(x4, CH + HALO, jnp.zeros((32, CH), jnp.float32))
     for j in range(4):
         fetches[j].wait()
-    pl.semaphore_wait(barrier, len(near))
-
-    for k in range(N_TAPS):
-        stage0(k)
-    signal(rounds.at[0], [at_z(1), at_z(-1), at_y(1), at_y(-1)])
+    fetch(stage.at[y], wbuf.at[PLAIN + y, xi, core, zl])
+    pl.semaphore_wait(barrier, 7)
+    signal(rounds.at[0], beside)
+
+    share0(0, 1)
+    share0(0, -1)
+    for k in range(PLAIN):
+        stage0(k, 1)
+        stage0(k, -1)
+    share0(1, 0)
+    share0(-1, 0)
+    pl.semaphore_wait(rounds.at[0], 6)
+    signal(rounds.at[1], [at_z(2), at_z(-2), at_x(2)])
+    share0(0, 2)
+    for k in range(PLAIN):
+        stage0(k, 2)
+    for dx, dz in ((2, 0), (1, 1), (1, -1), (-1, 1), (-1, -1)):
+        share0(dx, dz)
     fetches[4].wait()
     put(x4, 0, masked(fbuf[...], tm * CH))
-    for k in range(N_TAPS):
-        stage1(k)
-        if k == 4:
-            pl.semaphore_wait(rounds.at[0], 4)
-            signal(rounds.at[1], [at_z(2), at_z(-2)])
-    for k in range(WINDOW):
-        stage2(k)
-    pl.semaphore_wait(rounds.at[1], 2)
+    pl.semaphore_wait(rounds.at[1], 3)
     signal(rounds.at[2], [at_z(4), at_z(-4)])
+    for dx, dz in ((1, 2), (-1, 2), (2, 1), (2, -1), (2, 2)):
+        share0(dx, dz)
     fetches[5].wait()
     arrange_pos()
+    fetches[7].wait()
+    share1(0)
+    for k in range(PLAIN):
+        stage1(k)
     pl.semaphore_wait(rounds.at[2], 2)
     halo_copy = send(frames_ref.at[pl.ds(0, HALO)], halo, h_send, h_recv, before)
-
-    for step in range(N_TAPS + LAG5):
-        if step < N_TAPS:
-            stage3(step)
-        if step + WINDOW < N_TAPS:
-            stage2(step + WINDOW)
-        if step == N_TAPS - 1:
-            pos_start()
-        if 0 <= step - LAG4 < N_TAPS:
-            stage4(step - LAG4)
-        done = step - LAG5
-        if done >= 0:
-            stage5(done)
-            if done == 2:
-                halo_copy.wait_recv()
-                put(x4, CH, masked(halo[...], tm * CH + CH))
-                put(x5, 0, conv(x4, 0, 3, ROWS4))
-            if done == 5:
-                put(x6, 0, conv(x5, 3, 3, 128))
-            if done == 7:
-                put(x7, 0, conv(x6, 6, 2, 64))
+    pos_start()
+    share1(1)
+    share1(-1)
+    pass_on(0)
+    pass_on(1)
+    share1(2)
+    fetches[6].wait()
+    for by in (1, 3, 2):
+        lend(by)
+    for k in range(2, PLAIN):
+        pass_on(k)
+    flow(("q", 0), wbuf.at[shared, :, core], partner)
+    for k in range(PLAIN):
+        stage2(k)
+        if k == 4:
+            for j in range(3):
+                flows["p", j].wait_recv()
+            halo_copy.wait_recv()
+            put(x4, CH, masked(halo[...], tm * CH + CH))
+            put(x5, 0, conv(x4, 0, 3, ROWS4))
+    pos_forward(1)
+    for by in (1, 3, 2):
+        share2(by)
+    pos_forward(2)
+    for k in range(3, PLAIN):
+        flows["p", k].wait_recv()
+    put(x6, 0, conv(x5, 3, 3, 128))
+    for by in (0, 1, 3, 2):
+        flows["q", by].wait_recv()
+    put(x7, 0, conv(x6, 6, 2, 64))
     last = conv(x7, 8, 2, 32)
     normed = norm(last) * gain_ref[...] + nbias_ref[...]
-    nbuf[tm] = normed.astype(jnp.bfloat16)
+    nbuf[0] = normed.astype(jnp.bfloat16)
 
     act_flows = {}
 
-    def act_send(name, block, device):
-        j = len(act_flows)
-        act_flows[name] = send(block, block, a_send.at[j], a_recv.at[j], device)
-
     for j in (1, 3, 2):
-        act_send(("z", j), nbuf.at[tm], at_zh(j))
-    for by in (1, 2, 3):
-        act_send(("y", 0, by), nbuf.at[tm], at_y(by))
+        act_flows["z", j] = send(
+            nbuf.at[0], nbuf.at[j], a_send.at[j - 1], a_recv.at[j - 1], at_zh(j)
+        )
+    for by in (1, 3, 2):
+        flows["w", by].wait_recv()
+        flows["c", by].wait_recv()
+    row = lax.broadcasted_iota(jnp.int32, (32, GW), 0)
+
+    def project(j):
+        source = lax.rem(zh - j + 4, 4) * 4 + y
+        rows = nbuf[j]
+        for group in range(4):
+            hidden = lax.dot_general(
+                rows, pwbuf[group], (((1,), (1,)), ((), ())),
+                preferred_element_type=jnp.float32,
+            )
+            hidden = hidden + bbuf[group, pl.ds(0, 1), pl.ds(0, GW)].astype(jnp.float32)
+            hidden = jnp.where((source * 32 + row) * 320 < length, hidden, 0.0)
+            hidden = jnp.concatenate([hidden, jnp.zeros((32, 128 - GW), jnp.float32)], axis=1)
+            hidden = hidden.astype(jnp.bfloat16)
+            sbuf[j, group] = hidden
+            mine = hidden if group == 0 else jnp.where(group == y, hidden, mine)
+        for by in (1, 3, 2):
+            j_send = len(act_flows)
+            act_flows["y", j, by] = send(
+                sbuf.at[j, lax.rem(y + by, 4)], hbuf.at[source],
+                a_send.at[j_send], a_recv.at[j_send], at_y(by),
+            )
+        hbuf[source] = mine
+
+    project(0)
     pos_relay(0)
-    for j in (1, 2, 3):
-        pos_forward(j)
+    pos_forward(3)
+    pos_relay(1)
+    pos_relay(2)
+    pos_relay(3)
     for j in (1, 3, 2):
         act_flows["z", j].wait_recv()
-        block = nbuf.at[lax.rem(zh - j + 4, 4) * 4 + y]
-        for by in (1, 2, 3):
-            act_send(("y", j, by), block, at_y(by))
+        project(j)
     pos_swap(0)
-    for j in (1, 2, 3):
-        pos_relay(j)
-    fetches[6].wait()
+    pos_swap(1)
     for j in range(4):
         for by in (1, 2, 3):
             act_flows["y", j, by].wait_recv()
-
-    gathered = nbuf[...].reshape(CH, CH)
-    hidden = lax.dot_general(
-        gathered, pwbuf[...], (((1,), (1,)), ((), ())), preferred_element_type=jnp.float32
-    )
-    hidden = (hidden + pb_ref[...].astype(jnp.float32)).astype(jnp.bfloat16)
-    frame = lax.broadcasted_iota(jnp.int32, (CH, GW), 0)
-    hidden = jnp.where(frame * 320 < length, hidden.astype(jnp.float32), 0.0)
-    hf[pl.ds(64, CH), pl.ds(0, GW)] = hidden
-    for j in (1, 2, 3):
-        pos_swap(j)
+    hf[pl.ds(64, CH), :] = hbuf[...].reshape(CH, 128).astype(jnp.float32)
     for tap in range(16):
         x16[:, pl.ds(tap * 128, 128)] = hf[pl.ds(tap, 624), :].astype(jnp.bfloat16)
+    pos_swap(2)
+    pos_swap(3)
     for j in range(4):
         pos_flows["p", j].wait_recv()
     total = None
@@ -332,22 +387,26 @@
         out_specs=vmem,
         scratch_shapes=[
             pltpu.VMEM((N_TAPS, 4, 2, 4, 16, CH), jnp.bfloat16),
+            pltpu.VMEM((4, 16, CH), jnp.bfloat16),
             pltpu.VMEM((2, 2, 4, 2, 128, 512), jnp.bfloat16),
             pltpu.VMEM((CH, CH), jnp.bfloat16),
             pltpu.VMEM((4, GW * GW), jnp.bfloat16),
-            pltpu.VMEM((GW, CH), jnp.bfloat16),
+            pltpu.VMEM((4, GW, CH), jnp.bfloat16),
+            pltpu.VMEM((4, 16, 128), jnp.bfloat16),
             pltpu.VMEM((HALO, CH), jnp.bfloat16),
             pltpu.VMEM((4, CH + HALO + 32, 128), jnp.float32),
             pltpu.VMEM((4, ROWS4, 128), jnp.float32),
             pltpu.VMEM((4, 128, 128), jnp.float32),
             pltpu.VMEM((4, 64, 128), jnp.float32),
-            pltpu.VMEM((16, 32, CH), jnp.bfloat16),
+            pltpu.VMEM((4, 32, CH), jnp.bfloat16),
+            pltpu.VMEM((4, 4, 32, 128), jnp.bfloat16),
+            pltpu.VMEM((16, 32, 128), jnp.bfloat16),
             pltpu.VMEM((640, 128), jnp.float32),
             pltpu.VMEM((624, 2048), jnp.bfloat16),
             pltpu.VMEM((512, 128), jnp.float32),
-            dma((7,)),
-            dma((N_TAPS, 7)),
-            dma((N_TAPS, 7)),
+            dma((8,)),
+            dma((79,)),
+            dma((79,)),
             dma((19,)),
             dma((19,)),
             dma((15,)),

time: 73.3 us -> 64.6 us (0.88)
  the two profiles are of different devices: /device:TPU:97 before, /device:TPU:33 now
where the time goes in v3:
time: 64.6 us; the launch traced here: 64.5 us
  Pallas kernels  62.2 us (96%)
  local copies, waits for them, and re-layouts  1.56 us (2%)
  between operations  0.66 us (1%)
    pallas_call x1, Pallas kernels, local(): pl.pallas_call(kernel, out_shape=jax.ShapeDtypeStruct((GW, CH), jnp.bfloa...  62.2 us
    unnamed x1, local copies, waits for them, and re-layouts  1.56 us

profile of v3, /device:TPU:33, one launch (start us, length us, event | category | flops | bytes accessed | tf_op | source)
XLA Modules:
  0.0 64.5 jit_solution(1780676773145399686)
XLA Ops:
  0.7 62.2 %shard_map.118 = bf16[120,512]{1,0:T(8,128)(2,1)} custom-call(s32[1]{0:T(128)S(6)} %copy.14.len_ref, bf16[512,512]{1,0:T(8,128)(2,1)} %bitcast.7, bf16[3,16,512]{2,1,0:T(8,128)(2,1)} %w4_ref.1, bf16[3,16,512]{2,1,0:T(8,128)(2,1)} %w5_ref.1, bf16[2,16,512]{2,1,0:T(8,128)(2,1)} %w6_ref.1, bf16[2,16,512]{2,1,0:T(8,128)(2,1)} %w7_ref.1, f32[1,512]{1,0:T(1,128)} %bitcast.11, ...), custom_call_target="tpu_custom_call" | custom-call | tf_op jit(solution)/shard_map/pallas_call | solution.py:383
  62.9 1.6 %copy.15 = bf16[1,120,512]{2,1,0:T(8,128)(2,1)} copy(bf16[1,120,512]{2,1,0:T(8,128)(2,1)} %bitcast.8) | data formatting | bytes 245760

commit v4 on v3

--- a/solution.py
+++ b/solution.py
@@ -197,12 +197,17 @@
         pos_flows["x", j, -1].wait_recv()
         block = pos_block(lax.rem(xi - direction + 4, 4), lax.rem(zl - j + 4, 4))
         pos_send(("r", j), block, at_x(direction))
+        pos_share(j)
+
+    def pos_share(j):
+        for dx in (0, 1, -1):
+            block = pos_block(lax.rem(xi + dx + 4, 4), lax.rem(zl - j + 4, 4))
+            pos_send(("p", j, dx), block, partner)
 
     def pos_swap(j):
         pos_flows["r", j].wait_recv()
-        z = lax.rem(zl - j + 4, 4)
-        block = pbuf.at[:, core, z, :, pl.ds(0, GW)]
-        pos_send(("p", j), block, partner)
+        block = pos_block(lax.rem(xi + 2, 4), lax.rem(zl - j + 4, 4))
+        pos_send(("p", j, 2), block, partner)
 
     length = len_ref[0]
 
@@ -286,13 +291,12 @@
             halo_copy.wait_recv()
             put(x4, CH, masked(halo[...], tm * CH + CH))
             put(x5, 0, conv(x4, 0, 3, ROWS4))
-    pos_forward(1)
     for by in (1, 3, 2):
         share2(by)
-    pos_forward(2)
     for k in range(3, PLAIN):
         flows["p", k].wait_recv()
     put(x6, 0, conv(x5, 3, 3, 128))
+    pos_forward(1)
     for by in (0, 1, 3, 2):
         flows["q", by].wait_recv()
     put(x7, 0, conv(x6, 6, 2, 64))
@@ -311,37 +315,43 @@
         flows["c", by].wait_recv()
     row = lax.broadcasted_iota(jnp.int32, (32, GW), 0)
 
-    def project(j):
-        source = lax.rem(zh - j + 4, 4) * 4 + y
-        rows = nbuf[j]
+    def project(first, count):
+        rows = nbuf[pl.ds(first, count)].reshape(count * 32, CH)
+        mine = [None] * 4
         for group in range(4):
             hidden = lax.dot_general(
                 rows, pwbuf[group], (((1,), (1,)), ((), ())),
                 preferred_element_type=jnp.float32,
             )
             hidden = hidden + bbuf[group, pl.ds(0, 1), pl.ds(0, GW)].astype(jnp.float32)
-            hidden = jnp.where((source * 32 + row) * 320 < length, hidden, 0.0)
-            hidden = jnp.concatenate([hidden, jnp.zeros((32, 128 - GW), jnp.float32)], axis=1)
-            hidden = hidden.astype(jnp.bfloat16)
-            sbuf[j, group] = hidden
-            mine = hidden if group == 0 else jnp.where(group == y, hidden, mine)
-        for by in (1, 3, 2):
-            j_send = len(act_flows)
-            act_flows["y", j, by] = send(
-                sbuf.at[j, lax.rem(y + by, 4)], hbuf.at[source],
-                a_send.at[j_send], a_recv.at[j_send], at_y(by),
-            )
-        hbuf[source] = mine
-
-    project(0)
+            for j in range(first, first + count):
+                source = lax.rem(zh - j + 4, 4) * 4 + y
+                part = hidden[(j - first) * 32 : (j - first) * 32 + 32]
+                part = jnp.where((source * 32 + row) * 320 < length, part, 0.0)
+                part = jnp.concatenate([part, jnp.zeros((32, 128 - GW), jnp.float32)], axis=1)
+                part = part.astype(jnp.bfloat16)
+                sbuf[j, group] = part
+                mine[j] = part if group == 0 else jnp.where(group == y, part, mine[j])
+        for j in range(first, first + count):
+            source = lax.rem(zh - j + 4, 4) * 4 + y
+            for by in (1, 3, 2):
+                j_send = len(act_flows)
+                act_flows["y", j, by] = send(
+                    sbuf.at[j, lax.rem(y + by, 4)], hbuf.at[source],
+                    a_send.at[j_send], a_recv.at[j_send], at_y(by),
+                )
+            hbuf[source] = mine[j]
+
+    project(0, 1)
+    pos_forward(2)
+    pos_forward(3)
     pos_relay(0)
-    pos_forward(3)
     pos_relay(1)
     pos_relay(2)
     pos_relay(3)
     for j in (1, 3, 2):
         act_flows["z", j].wait_recv()
-        project(j)
+    project(1, 3)
     pos_swap(0)
     pos_swap(1)
     for j in range(4):
@@ -353,7 +363,8 @@
     pos_swap(2)
     pos_swap(3)
     for j in range(4):
-        pos_flows["p", j].wait_recv()
+        for dx in (0, 1, -1, 2):
+            pos_flows["p", j, dx].wait_recv()
     total = None
     for m in range(4):
         weight = jnp.concatenate(
@@ -407,8 +418,8 @@
             dma((8,)),
             dma((79,)),
             dma((79,)),
-            dma((19,)),
-            dma((19,)),
+            dma((31,)),
+            dma((31,)),
             dma((15,)),
             dma((15,)),
             dma,

time: 64.6 us -> 63.7 us (0.986)
  the two profiles are of different devices: /device:TPU:33 before, /device:TPU:65 now
where the time goes in v4:
time: 63.7 us; the launch traced here: 63.5 us
  Pallas kernels  61.3 us (96%)
  local copies, waits for them, and re-layouts  1.56 us (2%)
  between operations  0.66 us (1%)
    pallas_call x1, Pallas kernels, local(): pl.pallas_call(kernel, out_shape=jax.ShapeDtypeStruct((GW, CH), jnp.bfloa...  61.3 us
    unnamed x1, local copies, waits for them, and re-layouts  1.56 us

profile of v4, /device:TPU:65, one launch (start us, length us, event | category | flops | bytes accessed | tf_op | source)
XLA Modules:
  0.0 63.5 jit_solution(15087968574912213864)
XLA Ops:
  0.7 61.3 %shard_map.118 = bf16[120,512]{1,0:T(8,128)(2,1)} custom-call(s32[1]{0:T(128)S(6)} %copy.14.len_ref, bf16[512,512]{1,0:T(8,128)(2,1)} %bitcast.7, bf16[3,16,512]{2,1,0:T(8,128)(2,1)} %w4_ref.1, bf16[3,16,512]{2,1,0:T(8,128)(2,1)} %w5_ref.1, bf16[2,16,512]{2,1,0:T(8,128)(2,1)} %w6_ref.1, bf16[2,16,512]{2,1,0:T(8,128)(2,1)} %w7_ref.1, f32[1,512]{1,0:T(1,128)} %bitcast.11, ...), custom_call_target="tpu_custom_call" | custom-call | tf_op jit(solution)/shard_map/pallas_call | solution.py:394
  61.9 1.6 %copy.15 = bf16[1,120,512]{2,1,0:T(8,128)(2,1)} copy(bf16[1,120,512]{2,1,0:T(8,128)(2,1)} %bitcast.8) | data formatting | bytes 245760

commit v5 on v4

--- a/solution.py
+++ b/solution.py
@@ -263,10 +263,10 @@
     signal(rounds.at[2], [at_z(4), at_z(-4)])
     for dx, dz in ((1, 2), (-1, 2), (2, 1), (2, -1), (2, 2)):
         share0(dx, dz)
+    fetches[7].wait()
+    share1(0)
     fetches[5].wait()
     arrange_pos()
-    fetches[7].wait()
-    share1(0)
     for k in range(PLAIN):
         stage1(k)
     pl.semaphore_wait(rounds.at[2], 2)

time: 63.7 us -> 63.7 us (level)
  no operation moved by 1% of the time
where the time goes in v5:
time: 63.7 us; the launch traced here: 63.5 us
  Pallas kernels  61.3 us (96%)
  local copies, waits for them, and re-layouts  1.56 us (2%)
  between operations  0.66 us (1%)
    pallas_call x1, Pallas kernels, local(): pl.pallas_call(kernel, out_shape=jax.ShapeDtypeStruct((GW, CH), jnp.bfloa...  61.3 us
    unnamed x1, local copies, waits for them, and re-layouts  1.56 us

profile of v5, /device:TPU:65, one launch (start us, length us, event | category | flops | bytes accessed | tf_op | source)
XLA Modules:
  0.0 63.5 jit_solution(18431038812231673848)
XLA Ops:
  0.7 61.3 %shard_map.118 = bf16[120,512]{1,0:T(8,128)(2,1)} custom-call(s32[1]{0:T(128)S(6)} %copy.14.len_ref, bf16[512,512]{1,0:T(8,128)(2,1)} %bitcast.7, bf16[3,16,512]{2,1,0:T(8,128)(2,1)} %w4_ref.1, bf16[3,16,512]{2,1,0:T(8,128)(2,1)} %w5_ref.1, bf16[2,16,512]{2,1,0:T(8,128)(2,1)} %w6_ref.1, bf16[2,16,512]{2,1,0:T(8,128)(2,1)} %w7_ref.1, f32[1,512]{1,0:T(1,128)} %bitcast.11, ...), custom_call_target="tpu_custom_call" | custom-call | tf_op jit(solution)/shard_map/pallas_call | solution.py:394
  62.0 1.6 %copy.15 = bf16[1,120,512]{2,1,0:T(8,128)(2,1)} copy(bf16[1,120,512]{2,1,0:T(8,128)(2,1)} %bitcast.8) | data formatting | bytes 245760
